TPU v7x, 256 devices: a whole 4x4x8 slice. The times are simulated.
256 devices in a mesh: rows: 16 (over x, y_lo, core), cols: 16 (over z, y_hi).
Axes of the slice: x: 4, y: 4 (y_hi: 2, y_lo: 2; y = y_hi * 2 + y_lo), z: 8, core: 2. Of those that a mesh axis runs over, the one named last changes fastest.
Arguments:
- unary: float32 [21, 256, 2048], P(None, 'rows', 'cols'), may hold values from -8 to 300
- features: bfloat16 [64, 256, 2048], P(None, 'rows', 'cols'), may hold values from -9 to 9
- compat: float32 [21, 21], replicated, may hold values from -6 to 6
- grad_output: float32 [21, 256, 2048], P(None, 'rows', 'cols'), may hold values from -6 to 6
Outputs:
- unary_grad: float32 [21, 256, 2048], P(None, 'rows', 'cols')
- feature_grad: float32 [64, 256, 2048], P(None, 'rows', 'cols')
- compat_grad: float32 [21, 21], replicated
All inputs are finite; a program needn't handle non-finite values.
Results may differ from a plain program's by a relative error of at most 0.0003.
Values may be sent and summed in bfloat16 or wider, within the bound.
A program may use at most 128 MiB of HBM per device.

v0:
```python
import math

import jax
import jax.numpy as jnp
from jax import lax
from jax.sharding import PartitionSpec as P

ITERS = 2


THETA_PIXELS = 3.0
WINDOW_OFFSETS = [
    (row_step, col_step)
    for row_step in range(-3, 4)
    for col_step in range(-3, 4)
    if row_step != 0 or col_step != 0
]


def with_halo(block, sides, width):
    for axis, dim in sides:
        count = lax.axis_size(axis)
        forward = [(i, i + 1) for i in range(count - 1)]
        backward = [(target, source) for source, target in forward]
        low = lax.ppermute(
            lax.slice_in_dim(block, block.shape[dim] - width, None, axis=dim), axis, forward
        )
        high = lax.ppermute(lax.slice_in_dim(block, 0, width, axis=dim), axis, backward)
        block = jnp.concatenate([low, block, high], axis=dim)
    return block


def spatial_weight(row_step, col_step):
    return math.exp(
        -(row_step * row_step + col_step * col_step) / (2.0 * THETA_PIXELS * THETA_PIXELS)
    )


def shifted_view(padded, row_step, col_step, height, width_cells):
    return padded[
        :, 3 + row_step : 3 + row_step + height, 3 + col_step : 3 + col_step + width_cells
    ]


def affinity(padded_features):
    height = padded_features.shape[1] - 6
    width_cells = padded_features.shape[2] - 6
    center = shifted_view(padded_features, 0, 0, height, width_cells).astype(jnp.float32)
    factor = 1.0 / (2.0 * padded_features.shape[0])
    layers = []
    for row_step, col_step in WINDOW_OFFSETS:
        shifted = shifted_view(padded_features, row_step, col_step, height, width_cells).astype(
            jnp.float32
        )
        distance = jnp.sum((shifted - center) * (shifted - center), axis=0)
        layers.append(spatial_weight(row_step, col_step) * jnp.exp(-distance * factor))
    return jnp.stack(layers)


def message(kernel, padded):
    height = kernel.shape[1]
    width_cells = kernel.shape[2]
    total = jnp.zeros((padded.shape[0], height, width_cells), jnp.float32)
    for number, (row_step, col_step) in enumerate(WINDOW_OFFSETS):
        total = total + kernel[number][None] * shifted_view(
            padded, row_step, col_step, height, width_cells
        )
    return total


def pair_terms(grad_padded, prob_padded):
    height = grad_padded.shape[1] - 6
    width_cells = grad_padded.shape[2] - 6
    grad_center = shifted_view(grad_padded, 0, 0, height, width_cells)
    prob_center = shifted_view(prob_padded, 0, 0, height, width_cells)
    layers = []
    for row_step, col_step in WINDOW_OFFSETS:
        prob_shift = shifted_view(prob_padded, row_step, col_step, height, width_cells)
        grad_shift = shifted_view(grad_padded, row_step, col_step, height, width_cells)
        layers.append(jnp.sum(grad_center * prob_shift + grad_shift * prob_center, axis=0))
    return jnp.stack(layers)


def feature_term(coefs, kernel, padded_features):
    height = kernel.shape[1]
    width_cells = kernel.shape[2]
    center = shifted_view(padded_features, 0, 0, height, width_cells).astype(jnp.float32)
    factor = 1.0 / padded_features.shape[0]
    total = jnp.zeros(center.shape, jnp.float32)
    for number, (row_step, col_step) in enumerate(WINDOW_OFFSETS):
        shifted = shifted_view(padded_features, row_step, col_step, height, width_cells).astype(
            jnp.float32
        )
        weight_map = coefs[number] * kernel[number] * factor
        total = total + weight_map[None] * (shifted - center)
    return total


def mix(compat, values):
    return jnp.einsum("cd,dhw->chw", compat, values, precision=lax.Precision.HIGHEST)


def mix_back(compat, values):
    return jnp.einsum("cd,chw->dhw", compat, values, precision=lax.Precision.HIGHEST)


def outer_sum(left, right):
    return jnp.einsum("chw,dhw->cd", left, right, precision=lax.Precision.HIGHEST)


def softmax_grad(prob, cotangent):
    return prob * (cotangent - jnp.sum(cotangent * prob, axis=0, keepdims=True))


def on_device(unary, features, compat, grad_output):
    height = unary.shape[1]
    width_cells = unary.shape[2]
    total_pixels = height * lax.axis_size("rows") * width_cells * lax.axis_size("cols")
    reach = 0
    feat_wide = with_halo(features, (("rows", 1), ("cols", 2)), 3)
    cotangent = grad_output
    start_prob = jax.nn.softmax(unary, axis=0)
    kern_store = affinity(feat_wide)

    def kernel_at():
        return kern_store

    prob_list = [start_prob]
    pad_list = [reach]
    wide_list = []
    message_list = []
    for step in range(ITERS):
        current = prob_list[-1]
        prob_wide = with_halo(current, (("rows", 1), ("cols", 2)), 3)
        wide_pad = 3
        wide_list.append((prob_wide, wide_pad))
        out_pad = wide_pad - 3
        message_out = message(kernel_at(), prob_wide)
        message_list.append(message_out)
        logits = unary - mix(compat, message_out)
        next_prob = jax.nn.softmax(logits, axis=0)
        prob_list.append(next_prob)
        pad_list.append(out_pad)
    unary_sum = jnp.zeros(unary.shape, jnp.float32)
    compat_sum = jnp.zeros(compat.shape, jnp.float32)
    coefs = jnp.zeros((len(WINDOW_OFFSETS), height, width_cells), jnp.float32)
    for step in reversed(range(ITERS)):
        later_prob = prob_list[step + 1]
        logit_grad = softmax_grad(later_prob, cotangent)
        unary_sum = unary_sum + logit_grad
        compat_sum = compat_sum - outer_sum(logit_grad, message_list[step])
        msg_grad = -mix_back(compat, logit_grad)
        grad_wide = with_halo(msg_grad, (("rows", 1), ("cols", 2)), 3)
        cotangent = message(kernel_at(), grad_wide)
        prob_wide, wide_pad = wide_list[step]
        coefs = coefs + pair_terms(grad_wide, prob_wide)
    unary_grad = unary_sum + softmax_grad(prob_list[0], cotangent)
    feature_grad = feature_term(coefs, kernel_at(), feat_wide)
    compat_grad = lax.psum(compat_sum, ("rows", "cols")) / math.sqrt(total_pixels)
    return (unary_grad, feature_grad, compat_grad)


def solution(mesh):
    placed = (P(None, "rows", "cols"), P(None, "rows", "cols"), P(), P(None, "rows", "cols"))
    return jax.shard_map(
        on_device,
        mesh=mesh,
        in_specs=placed,
        out_specs=(P(None, "rows", "cols"), P(None, "rows", "cols"), P()),
        check_vma=False,
    )
```

profile of v0, /device:TPU:33, one launch (start us, length us, event | category | flops | bytes accessed | tf_op | source)
XLA Modules:
  0.0 314.2 jit_solution(16345287022579159694)
XLA Ops:
  3.7 3.8 %collective-permute-start.3 = (f32[21,3,128]{2,0,1:T(8,128)S(1)}, f32[21,3,128]{2,0,1:T(8,128)S(1)}, u32[]{:S(2)}, u32[]{:S(2)}) collective-permute-start(f32[21,3,128]{2,0,1:T(8,128)S(1)} %get-tuple-element.238), channel_id=1, source_target_pairs={{0,16},{16,32},{32,48},{48,64},{64,80},{80,96},{96,112},{112,128},... | collective-permute-start | bytes 96776 | tf_op jit(solution)/shard_map/ppermute | solution.py:25
  9.5 3.6 %collective-permute-start = (bf16[64,3,128]{2,1,0:T(4,128)(2,1)S(1)}, bf16[64,3,128]{2,1,0:T(4,128)(2,1)S(1)}, u32[]{:S(2)}, u32[]{:S(2)}) collective-permute-start(bf16[64,3,128]{2,1,0:T(4,128)(2,1)S(1)} %get-tuple-element.229), channel_id=1, source_target_pairs={{0,16},{16,32},{32,48},{48,64},{64,80},{80,96},{96,112},{112,128},... | collective-permute-start | bytes 147464 | tf_op jit(solution)/shard_map/ppermute | solution.py:25
  15.2 4.5 %collective-permute-start.5 = (f32[21,22,3]{2,0,1:T(8,128)S(1)}, f32[21,22,3]{2,0,1:T(8,128)S(1)}, u32[]{:S(2)}, u32[]{:S(2)}) collective-permute-start(f32[21,22,3]{2,0,1:T(8,128)S(1)} %get-tuple-element.227), channel_id=1, source_target_pairs={{0,1},{1,2},{2,3},{3,4},{4,5},{5,6},{6,7},{7,8},{8,9},{9,10},{10,1... | collective-permute-start | bytes 16640 | tf_op jit(solution)/shard_map/ppermute | solution.py:25
  19.8 3.2 %collective-permute-start.7 = (f32[21,22,3]{2,0,1:T(8,128)S(1)}, f32[21,22,3]{2,0,1:T(8,128)S(1)}, u32[]{:S(2)}, u32[]{:S(2)}) collective-permute-start(f32[21,22,3]{2,0,1:T(8,128)S(1)} %get-tuple-element.228), channel_id=1, source_target_pairs={{1,0},{2,1},{3,2},{4,3},{5,4},{6,5},{7,6},{8,7},{9,8},{10,9},{11,1... | collective-permute-start | bytes 16640 | tf_op jit(solution)/shard_map/ppermute | solution.py:28
  23.0 8.2 %collective-permute-done.5 = f32[21,22,3]{2,0,1:T(8,128)S(1)} collective-permute-done((f32[21,22,3]{2,0,1:T(8,128)S(1)}, f32[21,22,3]{2,0,1:T(8,128)S(1)}, u32[]{:S(2)}, u32[]{:S(2)}) %collective-permute-start.5) | collective-permute-done | bytes 5576 | tf_op jit(solution)/shard_map/ppermute | solution.py:25
  36.7 3.8 %collective-permute-start.2 = (bf16[64,22,3]{2,1,0:T(8,128)(2,1)S(1)}, bf16[64,22,3]{2,1,0:T(8,128)(2,1)S(1)}, u32[]{:S(2)}, u32[]{:S(2)}) collective-permute-start(bf16[64,22,3]{2,1,0:T(8,128)(2,1)S(1)} %get-tuple-element.212), channel_id=1, source_target_pairs={{0,1},{1,2},{2,3},{3,4},{4,5},{5,6},{6,7},{7,8},{8,9},{9,10},{10,1... | collective-permute-start | bytes 25352 | tf_op jit(solution)/shard_map/ppermute | solution.py:25
  40.5 15.3 %collective-permute-done.6 = bf16[64,22,3]{2,1,0:T(8,128)(2,1)S(1)} collective-permute-done((bf16[64,22,3]{2,1,0:T(8,128)(2,1)S(1)}, bf16[64,22,3]{2,1,0:T(8,128)(2,1)S(1)}, u32[]{:S(2)}, u32[]{:S(2)}) %collective-permute-start.6) | collective-permute-done | bytes 8480 | tf_op jit(solution)/shard_map/ppermute | solution.py:28
  83.4 5.8 %collective-permute-start.8 = (f32[21,3,128]{2,0,1:T(8,128)S(1)}, f32[21,3,128]{2,0,1:T(8,128)S(1)}, u32[]{:S(2)}, u32[]{:S(2)}) collective-permute-start(f32[21,3,128]{2,0,1:T(8,128)S(1)} %get-tuple-element.236), channel_id=1, source_target_pairs={{0,16},{16,32},{32,48},{48,64},{64,80},{80,96},{96,112},{112,128},... | collective-permute-start | bytes 96776 | tf_op jit(solution)/shard_map/ppermute | solution.py:25
  91.1 3.3 %collective-permute-done.9 = f32[21,3,128]{2,0,1:T(8,128)S(1)} collective-permute-done((f32[21,3,128]{2,0,1:T(8,128)S(1)}, f32[21,3,128]{2,0,1:T(8,128)S(1)}, u32[]{:S(2)}, u32[]{:S(2)}) %collective-permute-start.9) | collective-permute-done | bytes 32288 | tf_op jit(solution)/shard_map/ppermute | solution.py:28
  94.6 4.8 %collective-permute-start.10 = (f32[21,22,3]{2,0,1:T(8,128)S(1)}, f32[21,22,3]{2,0,1:T(8,128)S(1)}, u32[]{:S(2)}, u32[]{:S(2)}) collective-permute-start(f32[21,22,3]{2,0,1:T(8,128)S(1)} %get-tuple-element.223), channel_id=1, source_target_pairs={{0,1},{1,2},{2,3},{3,4},{4,5},{5,6},{6,7},{7,8},{8,9},{9,10},{10,1... | collective-permute-start | bytes 16640 | tf_op jit(solution)/shard_map/ppermute | solution.py:25
  102.5 7.3 %collective-permute-done.10 = f32[21,22,3]{2,0,1:T(8,128)S(1)} collective-permute-done((f32[21,22,3]{2,0,1:T(8,128)S(1)}, f32[21,22,3]{2,0,1:T(8,128)S(1)}, u32[]{:S(2)}, u32[]{:S(2)}) %collective-permute-start.10) | collective-permute-done | bytes 5576 | tf_op jit(solution)/shard_map/ppermute | solution.py:25
  118.5 4.6 %collective-permute-start.12 = (f32[21,3,128]{2,0,1:T(8,128)S(1)}, f32[21,3,128]{2,0,1:T(8,128)S(1)}, u32[]{:S(2)}, u32[]{:S(2)}) collective-permute-start(f32[21,3,128]{2,0,1:T(8,128)S(1)} %get-tuple-element.234), channel_id=1, source_target_pairs={{0,16},{16,32},{32,48},{48,64},{64,80},{80,96},{96,112},{112,128},... | collective-permute-start | bytes 96776 | tf_op jit(solution)/shard_map/ppermute | solution.py:25
  125.0 3.3 %collective-permute-done.13 = f32[21,3,128]{2,0,1:T(8,128)S(1)} collective-permute-done((f32[21,3,128]{2,0,1:T(8,128)S(1)}, f32[21,3,128]{2,0,1:T(8,128)S(1)}, u32[]{:S(2)}, u32[]{:S(2)}) %collective-permute-start.13) | collective-permute-done | bytes 32288 | tf_op jit(solution)/shard_map/ppermute | solution.py:28
  128.5 3.9 %collective-permute-start.14 = (f32[21,22,3]{2,0,1:T(8,128)S(1)}, f32[21,22,3]{2,0,1:T(8,128)S(1)}, u32[]{:S(2)}, u32[]{:S(2)}) collective-permute-start(f32[21,22,3]{2,0,1:T(8,128)S(1)} %get-tuple-element.219), channel_id=1, source_target_pairs={{0,1},{1,2},{2,3},{3,4},{4,5},{5,6},{6,7},{7,8},{8,9},{9,10},{10,1... | collective-permute-start | bytes 16640 | tf_op jit(solution)/shard_map/ppermute | solution.py:25
  132.4 3.8 %collective-permute-start.15 = (f32[21,22,3]{2,0,1:T(8,128)S(1)}, f32[21,22,3]{2,0,1:T(8,128)S(1)}, u32[]{:S(2)}, u32[]{:S(2)}) collective-permute-start(f32[21,22,3]{2,0,1:T(8,128)S(1)} %get-tuple-element.220), channel_id=1, source_target_pairs={{1,0},{2,1},{3,2},{4,3},{5,4},{6,5},{7,6},{8,7},{9,8},{10,9},{11,1... | collective-permute-start | bytes 16640 | tf_op jit(solution)/shard_map/ppermute | solution.py:28
  136.9 5.8 %collective-permute-done.14 = f32[21,22,3]{2,0,1:T(8,128)S(1)} collective-permute-done((f32[21,22,3]{2,0,1:T(8,128)S(1)}, f32[21,22,3]{2,0,1:T(8,128)S(1)}, u32[]{:S(2)}, u32[]{:S(2)}) %collective-permute-start.14) | collective-permute-done | bytes 5576 | tf_op jit(solution)/shard_map/ppermute | solution.py:25
  152.1 4.4 %add_reduce_fusion.48 = (f32[16,128]{1,0:T(8,128)}, f32[16,128]{1,0:T(8,128)}, f32[16,128]{1,0:T(8,128)}, f32[16,128]{1,0:T(8,128)}, f32[16,128]{1,0:T(8,128)}, ...) fusion(f32[21,16,128]{2,0,1:T(8,128)S(1)} %fusion.11, ...), kind=kLoop, calls=%fused_computation.349 | loop fusion | flops 5830656 | bytes 9657344 | tf_op jit(solution)/shard_map/reduce_sum | solution.py:80
  159.8 81.1 %psum.7 = f32[21,21]{1,0:T(8,128)S(1)} all-reduce(f32[21,21]{1,0:T(8,128)S(1)} %fusion.15), channel_id=1, replica_groups=mesh['rows'=16,'cols'=16] {'rows','cols'}, use_global_device_ids=true, to_apply=%region_153.0 | all-reduce | flops 441 | bytes 3528 | tf_op jit(solution)/shard_map/psum | solution.py:159
  257.8 3.8 %collective-permute-start.18 = (f32[21,22,3]{2,0,1:T(8,128)S(1)}, f32[21,22,3]{2,0,1:T(8,128)S(1)}, u32[]{:S(2)}, u32[]{:S(2)}) collective-permute-start(f32[21,22,3]{2,0,1:T(8,128)S(1)} %get-tuple-element.215), channel_id=1, source_target_pairs={{0,1},{1,2},{2,3},{3,4},{4,5},{5,6},{6,7},{7,8},{8,9},{9,10},{10,1... | collective-permute-start | bytes 16640 | tf_op jit(solution)/shard_map/ppermute | solution.py:25
  261.6 4.1 %collective-permute-start.19 = (f32[21,22,3]{2,0,1:T(8,128)S(1)}, f32[21,22,3]{2,0,1:T(8,128)S(1)}, u32[]{:S(2)}, u32[]{:S(2)}) collective-permute-start(f32[21,22,3]{2,0,1:T(8,128)S(1)} %get-tuple-element.216), channel_id=1, source_target_pairs={{1,0},{2,1},{3,2},{4,3},{5,4},{6,5},{7,6},{8,7},{9,8},{10,9},{11,1... | collective-permute-start | bytes 16640 | tf_op jit(solution)/shard_map/ppermute | solution.py:28
  266.0 6.7 %collective-permute-done.18 = f32[21,22,3]{2,0,1:T(8,128)S(1)} collective-permute-done((f32[21,22,3]{2,0,1:T(8,128)S(1)}, f32[21,22,3]{2,0,1:T(8,128)S(1)}, u32[]{:S(2)}, u32[]{:S(2)}) %collective-permute-start.18) | collective-permute-done | bytes 5576 | tf_op jit(solution)/shard_map/ppermute | solution.py:25
  272.7 3.5 %collective-permute-done.19 = f32[21,22,3]{2,0,1:T(8,128)S(1)} collective-permute-done((f32[21,22,3]{2,0,1:T(8,128)S(1)}, f32[21,22,3]{2,0,1:T(8,128)S(1)}, u32[]{:S(2)}, u32[]{:S(2)}) %collective-permute-start.19) | collective-permute-done | bytes 5576 | tf_op jit(solution)/shard_map/ppermute | solution.py:28
  290.9 13.9 %fusion.7 = f32[21,16,128]{2,0,1:T(8,128)S(1)} fusion(f32[21,16,128]{2,0,1:T(8,128)S(1)} %copy-done.10, f32[16,128]{1,0:T(8,128)} %fusion.19, f32[21,16,128]{2,1,0:T(8,128)} %param.7, f32[21,16,128]{2,0,1:T(8,128)} %copy-done.11, f32[16,128]{1,0:T(8,128)} %get-tuple-element.242, f32[16,128]{1,0:T(8,128)S(1)} %copy-done.13, f32[16,128]{1,0:T(8,128)S(1)} %reduce_max.27, ...), kind=kOutput, calls=%fused_computation.55 | output fusion | flops 9205780 | bytes 18972672 | tf_op jit(solution)/shard_map/sub | solution.py:112
  305.9 8.3 %multiply_add_fusion = f32[64,16,128]{2,1,0:T(8,128)} fusion(bf16[64,16,128]{2,1,0:T(8,128)(2,1)S(1)} %copy-done.6, bf16[64,3,128]{2,1,0:T(4,128)(2,1)S(1)} %collective-permute-done, f32[16,128]{1,0:T(8,128)} %get-tuple-element.162, f32[16,128]{1,0:T(8,128)} %get-tuple-element.163, f32[16,128]{1,0:T(8,128)} %get-tuple-element.164, ...), kind=kLoop, calls=%fused_computation.80 | loop fusion | flops 26345472 | bytes 13025280 | tf_op jit(solution)/shard_map/add | solution.py:95
  (516 shorter events, 99.3 us)
Async XLA Ops:
  3.7 11.4 %collective-permute-start.3 = (f32[21,3,128]{2,0,1:T(8,128)S(1)}, f32[21,3,128]{2,0,1:T(8,128)S(1)}, u32[]{:S(2)}, u32[]{:S(2)}) collective-permute-start(f32[21,3,128]{2,0,1:T(8,128)S(1)} %get-tuple-element.238), channel_id=1, source_target_pairs={{0,16},{16,32},{32,48},{48,64},{64,80},{80,96},{96,112},{112,128},... | collective-permute-start | bytes 96776 | tf_op jit(solution)/shard_map/ppermute | solution.py:25
  7.5 7.6 %collective-permute-start.4 = (f32[21,3,128]{2,0,1:T(8,128)S(1)}, f32[21,3,128]{2,0,1:T(8,128)S(1)}, u32[]{:S(2)}, u32[]{:S(2)}) collective-permute-start(f32[21,3,128]{2,0,1:T(8,128)S(1)} %get-tuple-element.239), channel_id=1, source_target_pairs={{16,0},{32,16},{48,32},{64,48},{80,64},{96,80},{112,96},{128,112},... | collective-permute-start | bytes 96776 | tf_op jit(solution)/shard_map/ppermute | solution.py:28
  9.5 23.8 %collective-permute-start = (bf16[64,3,128]{2,1,0:T(4,128)(2,1)S(1)}, bf16[64,3,128]{2,1,0:T(4,128)(2,1)S(1)}, u32[]{:S(2)}, u32[]{:S(2)}) collective-permute-start(bf16[64,3,128]{2,1,0:T(4,128)(2,1)S(1)} %get-tuple-element.229), channel_id=1, source_target_pairs={{0,16},{16,32},{32,48},{48,64},{64,80},{80,96},{96,112},{112,128},... | collective-permute-start | bytes 147464 | tf_op jit(solution)/shard_map/ppermute | solution.py:25
  13.1 20.1 %collective-permute-start.1 = (bf16[64,3,128]{2,1,0:T(4,128)(2,1)S(1)}, bf16[64,3,128]{2,1,0:T(4,128)(2,1)S(1)}, u32[]{:S(2)}, u32[]{:S(2)}) collective-permute-start(bf16[64,3,128]{2,1,0:T(4,128)(2,1)S(1)} %get-tuple-element.230), channel_id=1, source_target_pairs={{16,0},{32,16},{48,32},{64,48},{80,64},{96,80},{112,96},{128,112},... | collective-permute-start | bytes 147464 | tf_op jit(solution)/shard_map/ppermute | solution.py:28
  15.2 15.9 %collective-permute-start.5 = (f32[21,22,3]{2,0,1:T(8,128)S(1)}, f32[21,22,3]{2,0,1:T(8,128)S(1)}, u32[]{:S(2)}, u32[]{:S(2)}) collective-permute-start(f32[21,22,3]{2,0,1:T(8,128)S(1)} %get-tuple-element.227), channel_id=1, source_target_pairs={{0,1},{1,2},{2,3},{3,4},{4,5},{5,6},{6,7},{7,8},{8,9},{9,10},{10,1... | collective-permute-start | bytes 16640 | tf_op jit(solution)/shard_map/ppermute | solution.py:25
  19.8 13.3 %collective-permute-start.7 = (f32[21,22,3]{2,0,1:T(8,128)S(1)}, f32[21,22,3]{2,0,1:T(8,128)S(1)}, u32[]{:S(2)}, u32[]{:S(2)}) collective-permute-start(f32[21,22,3]{2,0,1:T(8,128)S(1)} %get-tuple-element.228), channel_id=1, source_target_pairs={{1,0},{2,1},{3,2},{4,3},{5,4},{6,5},{7,6},{8,7},{9,8},{10,9},{11,1... | collective-permute-start | bytes 16640 | tf_op jit(solution)/shard_map/ppermute | solution.py:28
  33.7 22.1 %collective-permute-start.6 = (bf16[64,22,3]{2,1,0:T(8,128)(2,1)S(1)}, bf16[64,22,3]{2,1,0:T(8,128)(2,1)S(1)}, u32[]{:S(2)}, u32[]{:S(2)}) collective-permute-start(bf16[64,22,3]{2,1,0:T(8,128)(2,1)S(1)} %get-tuple-element.211), channel_id=1, source_target_pairs={{1,0},{2,1},{3,2},{4,3},{5,4},{6,5},{7,6},{8,7},{9,8},{10,9},{11,1... | collective-permute-start | bytes 25352 | tf_op jit(solution)/shard_map/ppermute | solution.py:28
  36.7 19.1 %collective-permute-start.2 = (bf16[64,22,3]{2,1,0:T(8,128)(2,1)S(1)}, bf16[64,22,3]{2,1,0:T(8,128)(2,1)S(1)}, u32[]{:S(2)}, u32[]{:S(2)}) collective-permute-start(bf16[64,22,3]{2,1,0:T(8,128)(2,1)S(1)} %get-tuple-element.212), channel_id=1, source_target_pairs={{0,1},{1,2},{2,3},{3,4},{4,5},{5,6},{6,7},{7,8},{8,9},{9,10},{10,1... | collective-permute-start | bytes 25352 | tf_op jit(solution)/shard_map/ppermute | solution.py:25
  83.4 7.7 %collective-permute-start.8 = (f32[21,3,128]{2,0,1:T(8,128)S(1)}, f32[21,3,128]{2,0,1:T(8,128)S(1)}, u32[]{:S(2)}, u32[]{:S(2)}) collective-permute-start(f32[21,3,128]{2,0,1:T(8,128)S(1)} %get-tuple-element.236), channel_id=1, source_target_pairs={{0,16},{16,32},{32,48},{48,64},{64,80},{80,96},{96,112},{112,128},... | collective-permute-start | bytes 96776 | tf_op jit(solution)/shard_map/ppermute | solution.py:25
  89.2 5.3 %collective-permute-start.9 = (f32[21,3,128]{2,0,1:T(8,128)S(1)}, f32[21,3,128]{2,0,1:T(8,128)S(1)}, u32[]{:S(2)}, u32[]{:S(2)}) collective-permute-start(f32[21,3,128]{2,0,1:T(8,128)S(1)} %get-tuple-element.237), channel_id=1, source_target_pairs={{16,0},{32,16},{48,32},{64,48},{80,64},{96,80},{112,96},{128,112},... | collective-permute-start | bytes 96776 | tf_op jit(solution)/shard_map/ppermute | solution.py:28
  94.6 15.2 %collective-permute-start.10 = (f32[21,22,3]{2,0,1:T(8,128)S(1)}, f32[21,22,3]{2,0,1:T(8,128)S(1)}, u32[]{:S(2)}, u32[]{:S(2)}) collective-permute-start(f32[21,22,3]{2,0,1:T(8,128)S(1)} %get-tuple-element.223), channel_id=1, source_target_pairs={{0,1},{1,2},{2,3},{3,4},{4,5},{5,6},{6,7},{7,8},{8,9},{9,10},{10,1... | collective-permute-start | bytes 16640 | tf_op jit(solution)/shard_map/ppermute | solution.py:25
  99.4 12.0 %collective-permute-start.11 = (f32[21,22,3]{2,0,1:T(8,128)S(1)}, f32[21,22,3]{2,0,1:T(8,128)S(1)}, u32[]{:S(2)}, u32[]{:S(2)}) collective-permute-start(f32[21,22,3]{2,0,1:T(8,128)S(1)} %get-tuple-element.224), channel_id=1, source_target_pairs={{1,0},{2,1},{3,2},{4,3},{5,4},{6,5},{7,6},{8,7},{9,8},{10,9},{11,1... | collective-permute-start | bytes 16640 | tf_op jit(solution)/shard_map/ppermute | solution.py:28
  118.5 6.5 %collective-permute-start.12 = (f32[21,3,128]{2,0,1:T(8,128)S(1)}, f32[21,3,128]{2,0,1:T(8,128)S(1)}, u32[]{:S(2)}, u32[]{:S(2)}) collective-permute-start(f32[21,3,128]{2,0,1:T(8,128)S(1)} %get-tuple-element.234), channel_id=1, source_target_pairs={{0,16},{16,32},{32,48},{48,64},{64,80},{80,96},{96,112},{112,128},... | collective-permute-start | bytes 96776 | tf_op jit(solution)/shard_map/ppermute | solution.py:25
  123.0 5.3 %collective-permute-start.13 = (f32[21,3,128]{2,0,1:T(8,128)S(1)}, f32[21,3,128]{2,0,1:T(8,128)S(1)}, u32[]{:S(2)}, u32[]{:S(2)}) collective-permute-start(f32[21,3,128]{2,0,1:T(8,128)S(1)} %get-tuple-element.235), channel_id=1, source_target_pairs={{16,0},{32,16},{48,32},{64,48},{80,64},{96,80},{112,96},{128,112},... | collective-permute-start | bytes 96776 | tf_op jit(solution)/shard_map/ppermute | solution.py:28
  128.5 14.3 %collective-permute-start.14 = (f32[21,22,3]{2,0,1:T(8,128)S(1)}, f32[21,22,3]{2,0,1:T(8,128)S(1)}, u32[]{:S(2)}, u32[]{:S(2)}) collective-permute-start(f32[21,22,3]{2,0,1:T(8,128)S(1)} %get-tuple-element.219), channel_id=1, source_target_pairs={{0,1},{1,2},{2,3},{3,4},{4,5},{5,6},{6,7},{7,8},{8,9},{9,10},{10,1... | collective-permute-start | bytes 16640 | tf_op jit(solution)/shard_map/ppermute | solution.py:25
  132.4 12.9 %collective-permute-start.15 = (f32[21,22,3]{2,0,1:T(8,128)S(1)}, f32[21,22,3]{2,0,1:T(8,128)S(1)}, u32[]{:S(2)}, u32[]{:S(2)}) collective-permute-start(f32[21,22,3]{2,0,1:T(8,128)S(1)} %get-tuple-element.220), channel_id=1, source_target_pairs={{1,0},{2,1},{3,2},{4,3},{5,4},{6,5},{7,6},{8,7},{9,8},{10,9},{11,1... | collective-permute-start | bytes 16640 | tf_op jit(solution)/shard_map/ppermute | solution.py:28
  158.6 98.9 %copy-start.125 = (f32[16,128]{1,0:T(8,128)S(1)}, f32[16,128]{1,0:T(8,128)}, u32[]{:S(2)}) copy-start(f32[16,128]{1,0:T(8,128)} %get-tuple-element.14) | copy-start | bytes 24580
  158.7 98.9 %copy-start.130 = (f32[16,128]{1,0:T(8,128)S(1)}, f32[16,128]{1,0:T(8,128)}, u32[]{:S(2)}) copy-start(f32[16,128]{1,0:T(8,128)} %get-tuple-element.8) | copy-start | bytes 24580
  158.7 98.9 %copy-start.129 = (f32[16,128]{1,0:T(8,128)S(1)}, f32[16,128]{1,0:T(8,128)}, u32[]{:S(2)}) copy-start(f32[16,128]{1,0:T(8,128)} %get-tuple-element.7) | copy-start | bytes 24580
  158.7 98.9 %copy-start.128 = (f32[16,128]{1,0:T(8,128)S(1)}, f32[16,128]{1,0:T(8,128)}, u32[]{:S(2)}) copy-start(f32[16,128]{1,0:T(8,128)} %get-tuple-element.6) | copy-start | bytes 24580
  241.5 16.1 %collective-permute-start.16 = (f32[21,3,128]{2,0,1:T(8,128)S(1)}, f32[21,3,128]{2,0,1:T(8,128)S(1)}, u32[]{:S(2)}, u32[]{:S(2)}) collective-permute-start(f32[21,3,128]{2,0,1:T(8,128)S(1)} %get-tuple-element.232), channel_id=1, source_target_pairs={{0,16},{16,32},{32,48},{48,64},{64,80},{80,96},{96,112},{112,128},... | collective-permute-start | bytes 96776 | tf_op jit(solution)/shard_map/ppermute | solution.py:25
  243.5 14.2 %collective-permute-start.17 = (f32[21,3,128]{2,0,1:T(8,128)S(1)}, f32[21,3,128]{2,0,1:T(8,128)S(1)}, u32[]{:S(2)}, u32[]{:S(2)}) collective-permute-start(f32[21,3,128]{2,0,1:T(8,128)S(1)} %get-tuple-element.233), channel_id=1, source_target_pairs={{16,0},{32,16},{48,32},{64,48},{80,64},{96,80},{112,96},{128,112},... | collective-permute-start | bytes 96776 | tf_op jit(solution)/shard_map/ppermute | solution.py:28
  257.8 14.9 %collective-permute-start.18 = (f32[21,22,3]{2,0,1:T(8,128)S(1)}, f32[21,22,3]{2,0,1:T(8,128)S(1)}, u32[]{:S(2)}, u32[]{:S(2)}) collective-permute-start(f32[21,22,3]{2,0,1:T(8,128)S(1)} %get-tuple-element.215), channel_id=1, source_target_pairs={{0,1},{1,2},{2,3},{3,4},{4,5},{5,6},{6,7},{7,8},{8,9},{9,10},{10,1... | collective-permute-start | bytes 16640 | tf_op jit(solution)/shard_map/ppermute | solution.py:25
  261.6 14.6 %collective-permute-start.19 = (f32[21,22,3]{2,0,1:T(8,128)S(1)}, f32[21,22,3]{2,0,1:T(8,128)S(1)}, u32[]{:S(2)}, u32[]{:S(2)}) collective-permute-start(f32[21,22,3]{2,0,1:T(8,128)S(1)} %get-tuple-element.216), channel_id=1, source_target_pairs={{1,0},{2,1},{3,2},{4,3},{5,4},{6,5},{7,6},{8,7},{9,8},{10,9},{11,1... | collective-permute-start | bytes 16640 | tf_op jit(solution)/shard_map/ppermute | solution.py:28
  (152 other events, 6748.9 us)
where the time goes:
time: 319 us; the launch traced here: 314 us
  other arithmetic  84.1 us (26%)
  blocking collectives  81.1 us (25%)
  starting transfers between devices  67.7 us (21%)
  waiting for transfers between devices  59.5 us (19%)
  local copies, waits for them, and re-layouts  14.4 us (5%)
  between operations  3.99 us (1%)
  matrix products  3.54 us (1%)
    psum x1, blocking collectives, on_device(): lax.psum(compat_sum, ('rows', 'cols')) / math.sqrt(total_pixels)  81.1 us
    ppermute x10, starting transfers between devices, with_halo(): lax.ppermute(lax.slice_in_dim(block, block.shape[dim] - width, None, axis...  40.5 us
    ppermute x10, waiting for transfers between devices, with_halo(): lax.ppermute(lax.slice_in_dim(block, 0, width, axis=dim), axis, backward)  31.4 us
    ppermute x10, waiting for transfers between devices, with_halo(): lax.ppermute(lax.slice_in_dim(block, block.shape[dim] - width, None, axis...  28.1 us
    ppermute x10, starting transfers between devices, with_halo(): lax.ppermute(lax.slice_in_dim(block, 0, width, axis=dim), axis, backward)  27.2 us
    reduce_sum x16, other arithmetic, pair_terms(): jnp.sum(grad_center * prob_shift + grad_shift * prob_center, axis=0)  16.8 us
    mul x24, other arithmetic, affinity(): spatial_weight(row_step, col_step) * jnp.exp(-distance * factor)  14 us
    sub x1, other arithmetic, softmax_grad(): return prob * (cotangent - jnp.sum(cotangent * prob, axis=0, keepdims=True))  13.9 us
  transfers between devices with their start and end apart: 20, of which 11 were waited for; matrix products, arithmetic and copies ran while one was open for 4% of the time, Pallas kernels for 0%

commit v1 on v0

v1 whole, which is shorter than its diff:
```python
import functools
import math

import jax
import jax.numpy as jnp
from jax import lax
from jax.experimental import pallas as pl
from jax.experimental.pallas import tpu as pltpu
from jax.sharding import PartitionSpec as P

REACH = 3
SPAN = 2 * REACH + 1
THETA_PIXELS = 3.0
MESH = pl.DeviceIdType.MESH
LANES = 128
TOP = 8
PLANE = 32
WIN = 24
F_GROUP = 16
PHASES = 4
HALF = 8

ROUTES = (
    (-1, 0, 1),
    (1, 0, 0),
    (0, -1, 3),
    (0, 1, 2),
    (-1, -1, 7),
    (-1, 1, 5),
    (1, -1, 6),
    (1, 1, 4),
)


def kernel(
    n_rows, n_cols, classes, feats,
    u_hbm, f_hbm, cm, g_hbm,
    ug_ref, fg_ref, cg_ref,
    u_v, g_v, f_v, f_plane, plane, f_shift, shift, kern, coef,
    prob, msg, lgrad,
    f_rows_f32, f_srow, f_rrow, f_sstrip, f_rstrip, f_strip,
    srow, rrow, sstrip, rstrip,
    ar_one, ar_two,
    in_sem, f_ssem, f_rsem, ssem, rsem, ar_ssem, ar_rsem,
):
    f32 = jnp.float32
    height = u_v.shape[1]
    r = lax.axis_index("rows")
    c = lax.axis_index("cols")
    lane = lax.broadcasted_iota(jnp.int32, (1, LANES), 1)
    lane_group = lane // 6
    from_left = (lane % 6) < 3

    loads = [
        pltpu.make_async_copy(f_hbm, f_v, in_sem.at[0]),
        pltpu.make_async_copy(u_hbm, u_v, in_sem.at[1]),
        pltpu.make_async_copy(g_hbm, g_v, in_sem.at[2]),
    ]
    for load in loads:
        load.start()

    def inside(dr, dc):
        ok = None
        for pos, step, size in ((r, dr, n_rows), (c, dc, n_cols)):
            if step:
                here = (pos > 0) if step < 0 else (pos < size - 1)
                ok = here if ok is None else jnp.logical_and(ok, here)
        return ok

    def target(dr, dc):
        return {"rows": r + dr, "cols": c + dc}

    @pl.when(r == 0)
    def _():
        f_rrow[0] = jnp.zeros_like(f_rrow[0])
        for k in range(PHASES):
            rrow[k, 0] = jnp.zeros_like(rrow[k, 0])
        for side in range(2):
            f_rstrip[side, 0] = jnp.zeros_like(f_rstrip[side, 0])
            for k in range(PHASES):
                rstrip[k, side, 0:HALF] = jnp.zeros((HALF, LANES), f32)

    @pl.when(r == n_rows - 1)
    def _():
        f_rrow[1] = jnp.zeros_like(f_rrow[1])
        for k in range(PHASES):
            rrow[k, 1] = jnp.zeros_like(rrow[k, 1])
        for side in range(2):
            f_rstrip[side, 2] = jnp.zeros_like(f_rstrip[side, 2])
            for k in range(PHASES):
                rstrip[k, side, PLANE - HALF:PLANE] = jnp.zeros((HALF, LANES), f32)

    for side, edge in ((0, 0), (1, n_cols - 1)):
        @pl.when(c == edge)
        def _(side=side):
            f_rstrip[side] = jnp.zeros_like(f_rstrip[side])
            for k in range(PHASES):
                rstrip[k, side] = jnp.zeros((PLANE, LANES), f32)

    barrier = pltpu.get_barrier_semaphore()
    for k in range(1, n_rows):
        pl.semaphore_signal(barrier, inc=1, device_id={"rows": lax.rem(r + k, n_rows), "cols": c}, device_id_type=MESH)
    for k in range(1, n_cols):
        pl.semaphore_signal(barrier, inc=1, device_id={"rows": r, "cols": lax.rem(c + k, n_cols)}, device_id_type=MESH)
    for dr, dc, _ in ROUTES[4:]:
        there = {"rows": lax.rem(r + dr + n_rows, n_rows), "cols": lax.rem(c + dc + n_cols, n_cols)}
        pl.semaphore_signal(barrier, inc=1, device_id=there, device_id_type=MESH)

    def pack_rows(source, count, base_row, dst):
        for ch in range(count):
            dst[3 * ch:3 * ch + 3, :] = source[ch, base_row:base_row + 3, :]

    loads[0].wait()
    f_plane[:, TOP:TOP + height, :] = f_v[...].astype(f32)
    for side, base_row in ((0, TOP), (1, TOP + height - 3)):
        pack_rows(f_plane, feats, base_row, f_rows_f32)
        f_srow[side] = f_rows_f32[...].astype(jnp.bfloat16)
    for group in range(feats // F_GROUP):
        tile = jnp.zeros((height, LANES), f32)
        for k in range(F_GROUP):
            turned = pltpu.roll(f_plane[group * F_GROUP + k, TOP:TOP + height, :], 6 * k + 3, 1)
            tile = jnp.where(lane_group == k, turned, tile)
        f_sstrip[group] = tile.astype(jnp.bfloat16)

    def softmax(values):
        top = jnp.max(values, axis=0, keepdims=True)
        grown = jnp.exp(values - top)
        return grown / jnp.sum(grown, axis=0, keepdims=True)

    def pack(k, ref):
        plane[:, TOP:TOP + height, :] = ref[...]
        tile = jnp.zeros((height, LANES), f32)
        for ch in range(classes):
            turned = pltpu.roll(ref[ch], (6 * ch + 3) % LANES, 1)
            tile = jnp.where(lane_group == ch, turned, tile)
        sstrip[k] = tile
        pack_rows(plane, classes, TOP, srow.at[k, 0])
        pack_rows(plane, classes, TOP + height - 3, srow.at[k, 1])

    def field_copy(k, way):
        dr, dc, slot = ROUTES[way]
        if dc == 0:
            src = srow.at[k, 0 if dr < 0 else 1]
            dst = rrow.at[k, slot]
        else:
            side = 1 if dc < 0 else 0
            if dr == 0:
                src = sstrip.at[k]
                dst = rstrip.at[k, side, pl.ds(HALF, height)]
            elif dr < 0:
                src = sstrip.at[k, pl.ds(0, HALF)]
                dst = rstrip.at[k, side, pl.ds(HALF + height, HALF)]
            else:
                src = sstrip.at[k, pl.ds(height - HALF, HALF)]
                dst = rstrip.at[k, side, pl.ds(0, HALF)]
        return pltpu.make_async_remote_copy(
            src_ref=src, dst_ref=dst, send_sem=ssem.at[k, way], recv_sem=rsem.at[k, way],
            device_id=target(dr, dc), device_id_type=MESH,
        )

    def feature_copy(way):
        dr, dc, slot = ROUTES[way]
        if dc == 0:
            src = f_srow.at[0 if dr < 0 else 1]
            dst = f_rrow.at[slot]
        else:
            src = f_sstrip
            dst = f_rstrip.at[1 if dc < 0 else 0, 1 - dr]
        return pltpu.make_async_remote_copy(
            src_ref=src, dst_ref=dst, send_sem=f_ssem.at[way], recv_sem=f_rsem.at[way],
            device_id=target(dr, dc), device_id_type=MESH,
        )

    def each_way(make, act):
        for way, (dr, dc, _) in enumerate(ROUTES):
            if act == "start":
                @pl.when(inside(dr, dc))
                def _(way=way):
                    make(way).start()
            elif act == "recv":
                @pl.when(inside(-dr, -dc))
                def _(way=way):
                    make(way).wait_recv()
            else:
                @pl.when(inside(dr, dc))
                def _(way=way):
                    make(way).wait_send()

    loads[1].wait()
    prob[0] = softmax(u_v[...])
    pack(0, prob.at[0])
    loads[2].wait()
    pl.semaphore_wait(barrier, n_rows - 1 + n_cols - 1 + 4)
    each_way(feature_copy, "start")
    each_way(functools.partial(field_copy, 0), "start")

    def turn(edge, own, dst, ch):
        for b in range(-REACH, REACH + 1):
            if b == 0:
                dst[b + REACH, ch] = own
            elif b > 0:
                dst[b + REACH, ch] = pltpu.roll(jnp.where(lane < b, edge, own), LANES - b, 1)
            else:
                dst[b + REACH, ch] = pltpu.roll(jnp.where(lane >= LANES + b, edge, own), -b, 1)

    each_way(feature_copy, "recv")
    for side, base_row in ((0, TOP - 3), (1, TOP + height)):
        f_rows_f32[...] = f_rrow[side].astype(f32)
        for ch in range(feats):
            f_plane[ch, base_row:base_row + 3, :] = f_rows_f32[3 * ch:3 * ch + 3, :]
    for group in range(feats // F_GROUP):
        for part in range(3):
            both = jnp.where(
                from_left, f_rstrip[0, part, group].astype(f32), f_rstrip[1, part, group].astype(f32)
            )
            f_strip[group, part * height:(part + 1) * height] = both
    for group in range(feats // F_GROUP):
        strip = f_strip[group, height - 3:height - 3 + WIN]

        def f_turn(k, carry, group=group):
            ch = group * F_GROUP + k
            edge = pltpu.roll(f_strip[group, height - 3:height - 3 + WIN], LANES - 3 - 6 * k, 1)
            turn(edge, f_plane[ch, TOP - 3:TOP - 3 + WIN, :], f_shift, ch)
            return carry

        lax.fori_loop(0, F_GROUP, f_turn, 0)

    factor = 1.0 / (2.0 * feats)
    spread = 1.0 / (2.0 * THETA_PIXELS * THETA_PIXELS)

    def rows_at(a):
        return slice(a, a + height)

    def affinity(bi, carry):
        def channels(i, acc):
            for extra in range(4):
                ch = 4 * i + extra
                center = f_shift[REACH, ch, rows_at(REACH), :]
                new = []
                for a in range(SPAN):
                    gap = f_shift[bi, ch, rows_at(a), :] - center
                    new.append(acc[a] + gap * gap)
                acc = tuple(new)
            return acc

        zero = jnp.zeros((height, LANES), f32)
        acc = lax.fori_loop(0, feats // 4, channels, (zero,) * SPAN)
        step = (bi - REACH).astype(f32)
        for a in range(SPAN):
            away = ((a - REACH) * (a - REACH) + step * step) * spread
            kern[bi * SPAN + a] = jnp.exp(-acc[a] * factor - away)
        return carry

    lax.fori_loop(0, SPAN, affinity, 0)
    kern[REACH * SPAN + REACH] = jnp.zeros((height, LANES), f32)

    def arrive(k):
        each_way(functools.partial(field_copy, k), "recv")
        for ch in range(classes):
            plane[ch, TOP - 3:TOP, :] = rrow[k, 0, 3 * ch:3 * ch + 3, :]
            plane[ch, TOP + height:TOP + height + 3, :] = rrow[k, 1, 3 * ch:3 * ch + 3, :]
        strip = jnp.where(from_left, rstrip[k, 0, TOP - 3:TOP - 3 + WIN], rstrip[k, 1, TOP - 3:TOP - 3 + WIN])

        def f_turn(i, carry):
            for extra in range(3):
                ch = 3 * i + extra
                edge = pltpu.roll(strip, LANES - 3 - 6 * ch, 1)
                turn(edge, plane[ch, TOP - 3:TOP - 3 + WIN, :], shift.at[k], ch)
            return carry

        lax.fori_loop(0, classes // 3, f_turn, 0)

    def spread_out(k, dst):
        for block in range(classes // 7):
            chans = slice(7 * block, 7 * block + 7)

            def step(bi, acc):
                for a in range(SPAN):
                    acc = acc + kern[bi * SPAN + a][None] * shift[k, bi, chans, rows_at(a), :]
                return acc

            dst[chans] = lax.fori_loop(0, SPAN, step, jnp.zeros((7, height, LANES), f32))

    def mix(transposed, source, finish):
        def one(ch, carry):
            acc = jnp.zeros((height, LANES), f32)
            for d in range(classes):
                weight = cm[d, ch] if transposed else cm[ch, d]
                acc = acc + weight * source[d]
            finish(ch, acc)
            return carry

        lax.fori_loop(0, classes, one, 0)

    def set_logits(t):
        def finish(ch, acc):
            prob[t, ch] = u_v[ch] - acc
        return finish

    def set_msg_grad(ch, acc):
        plane[ch, TOP:TOP + height, :] = -acc
        prob[PHASES - 1, ch] = -acc

    def softmax_grad(value, cotangent):
        return value * (cotangent - jnp.sum(cotangent * value, axis=0, keepdims=True))

    arrive(0)
    spread_out(0, msg.at[0])
    mix(False, msg.at[0], set_logits(1))
    prob[1] = softmax(prob[1])
    pack(1, prob.at[1])
    each_way(functools.partial(field_copy, 1), "start")
    arrive(1)
    spread_out(1, msg.at[1])
    mix(False, msg.at[1], set_logits(2))
    prob[2] = softmax(prob[2])

    lgrad[1] = softmax_grad(prob[2], g_v[...])
    mix(True, lgrad.at[1], set_msg_grad)
    pack(2, prob.at[PHASES - 1])
    each_way(functools.partial(field_copy, 2), "start")

    def by_pixel(ref):
        return jnp.concatenate([ref[:, y, :] for y in range(height)], axis=1)

    def outer(t):
        return lax.dot_general(
            by_pixel(lgrad.at[t]), by_pixel(msg.at[t]), (((1,), (1,)), ((), ())),
            precision=lax.Precision.HIGHEST, preferred_element_type=f32,
        )

    total = outer(1)
    arrive(2)
    spread_out(2, ug_ref)

    lgrad[0] = softmax_grad(prob[1], ug_ref[...])
    mix(True, lgrad.at[0], set_msg_grad)
    pack(3, prob.at[PHASES - 1])
    each_way(functools.partial(field_copy, 3), "start")

    pixels = height * n_rows * LANES * n_cols
    total = (total + outer(0)) * (-1.0 / math.sqrt(pixels))
    ar_one[r, 0:classes, 0:classes] = total

    def reduce_copy(stage, k):
        buf = (ar_one, ar_two)[stage]
        size, pos = ((n_rows, r), (n_cols, c))[stage]
        there = lax.rem(pos + k, size)
        device = {"rows": there, "cols": c} if stage == 0 else {"rows": r, "cols": there}
        return pltpu.make_async_remote_copy(
            src_ref=buf.at[pos], dst_ref=buf.at[pos],
            send_sem=ar_ssem.at[stage, k], recv_sem=ar_rsem.at[stage, pos],
            device_id=device, device_id_type=MESH,
        )

    def reduce_arrival(stage, k):
        buf = (ar_one, ar_two)[stage]
        size, pos = ((n_rows, r), (n_cols, c))[stage]
        there = lax.rem(pos + k, size)
        device = {"rows": there, "cols": c} if stage == 0 else {"rows": r, "cols": there}
        return pltpu.make_async_remote_copy(
            src_ref=buf.at[pos], dst_ref=buf.at[there],
            send_sem=ar_ssem.at[stage, k], recv_sem=ar_rsem.at[stage, there],
            device_id=device, device_id_type=MESH,
        )

    for k in range(1, n_rows):
        reduce_copy(0, k).start()

    def pair(k_prob, k_grad, finish):
        def one(bi, carry):
            def channels(i, acc):
                for extra in range(3):
                    ch = 3 * i + extra
                    p_own = shift[k_prob, REACH, ch, rows_at(REACH), :]
                    m_own = shift[k_grad, REACH, ch, rows_at(REACH), :]
                    acc = tuple(
                        acc[a]
                        + m_own * shift[k_prob, bi, ch, rows_at(a), :]
                        + shift[k_grad, bi, ch, rows_at(a), :] * p_own
                        for a in range(SPAN)
                    )
                return acc

            zero = jnp.zeros((height, LANES), f32)
            acc = lax.fori_loop(0, classes // 3, channels, (zero,) * SPAN)
            for a in range(SPAN):
                finish(bi * SPAN + a, acc[a])
            return carry

        lax.fori_loop(0, SPAN, one, 0)

    def keep(o, value):
        coef[o] = value

    def close(o, value):
        coef[o] = (coef[o] + value) * kern[o] * (1.0 / feats)

    pair(1, 2, keep)

    for k in range(1, n_rows):
        reduce_arrival(0, k).wait_recv()
    ar_two[c] = jnp.sum(ar_one[...], axis=0)
    for k in range(1, n_cols):
        reduce_copy(1, k).start()

    arrive(3)
    spread_out(3, ug_ref)
    ug_ref[...] = lgrad[1] + lgrad[0] + softmax_grad(prob[0], ug_ref[...])
    pair(0, 3, close)

    def feature_block(i, carry):
        base = 4 * i
        chans = pl.ds(base, 4)
        center = f_shift[REACH, chans, rows_at(REACH), :]

        def step(bi, acc):
            for a in range(SPAN):
                acc = acc + coef[bi * SPAN + a][None] * (f_shift[bi, chans, rows_at(a), :] - center)
            return acc

        fg_ref[chans] = lax.fori_loop(0, SPAN, step, jnp.zeros((4, height, LANES), f32))
        return carry

    lax.fori_loop(0, feats // 4, feature_block, 0)

    for k in range(1, n_cols):
        reduce_arrival(1, k).wait_recv()
    cg_ref[...] = jnp.sum(ar_two[...], axis=0)[0:classes, 0:classes]

    each_way(feature_copy, "send")
    for k in range(PHASES):
        each_way(functools.partial(field_copy, k), "send")
    for stage, size in ((0, n_rows), (1, n_cols)):
        for k in range(1, size):
            reduce_copy(stage, k).wait_send()


def on_device(n_rows, n_cols, unary, features, compat, grad_output):
    classes, height, width = unary.shape
    feats = features.shape[0]
    f32 = jnp.float32
    vmem, dma = pltpu.VMEM, pltpu.SemaphoreType.DMA
    groups = feats // F_GROUP
    any_spec = pl.BlockSpec(memory_space=pl.ANY)
    vmem_spec = pl.BlockSpec(memory_space=pltpu.VMEM)
    return pl.pallas_call(
        functools.partial(kernel, n_rows, n_cols, classes, feats),
        out_shape=(
            jax.ShapeDtypeStruct((classes, height, width), f32),
            jax.ShapeDtypeStruct((feats, height, width), f32),
            jax.ShapeDtypeStruct((classes, classes), f32),
        ),
        in_specs=[any_spec, any_spec, pl.BlockSpec(memory_space=pltpu.SMEM), any_spec],
        out_specs=(vmem_spec, vmem_spec, vmem_spec),
        scratch_shapes=[
            vmem((classes, height, width), f32),
            vmem((classes, height, width), f32),
            vmem((feats, height, width), features.dtype),
            vmem((feats, PLANE, width), f32),
            vmem((classes, PLANE, width), f32),
            vmem((SPAN, feats, WIN, width), f32),
            vmem((PHASES, SPAN, classes, WIN, width), f32),
            vmem((SPAN * SPAN, height, width), f32),
            vmem((SPAN * SPAN, height, width), f32),
            vmem((PHASES, classes, height, width), f32),
            vmem((2, classes, height, width), f32),
            vmem((2, classes, height, width), f32),
            vmem((3 * feats, width), f32),
            vmem((2, 3 * feats, width), jnp.bfloat16),
            vmem((2, 3 * feats, width), jnp.bfloat16),
            vmem((groups, height, width), jnp.bfloat16),
            vmem((2, 3, groups, height, width), jnp.bfloat16),
            vmem((groups, 3 * height, width), f32),
            vmem((PHASES, 2, 64, width), f32),
            vmem((PHASES, 2, 64, width), f32),
            vmem((PHASES, height, width), f32),
            vmem((PHASES, 2, PLANE, width), f32),
            vmem((n_rows, 24, width), f32),
            vmem((n_cols, 24, width), f32),
            dma((3,)), dma((8,)), dma((8,)), dma((PHASES, 8)), dma((PHASES, 8)),
            dma((2, max(n_rows, n_cols))), dma((2, max(n_rows, n_cols))),
        ],
        compiler_params=pltpu.CompilerParams(collective_id=0, has_side_effects=True, vmem_limit_bytes=60 * 1024 * 1024),
        name="crf_backward",
    )(unary, features, compat, grad_output)


def solution(mesh):
    placed = (P(None, "rows", "cols"), P(None, "rows", "cols"), P(), P(None, "rows", "cols"))
    return jax.shard_map(
        functools.partial(on_device, mesh.shape["rows"], mesh.shape["cols"]),
        mesh=mesh,
        in_specs=placed,
        out_specs=(P(None, "rows", "cols"), P(None, "rows", "cols"), P()),
        check_vma=False,
    )
```

time: 319 us -> 68.8 us (0.22)
  the two profiles are of different devices: /device:TPU:33 before, /device:TPU:1 now
where the time goes in v1:
time: 68.8 us; the launch traced here: 68.6 us
  Pallas kernels  63.8 us (93%)
  local copies, waits for them, and re-layouts  4.08 us (6%)
    pallas_call x1, Pallas kernels, on_device(): pl.pallas_call(functools.partial(kernel, n_rows, n_cols, classes, feats),...  63.8 us
    unnamed x5, local copies, waits for them, and re-layouts  4.08 us

profile of v1, /device:TPU:1, one launch (start us, length us, event | category | flops | bytes accessed | tf_op | source)
XLA Modules:
  0.0 68.6 jit_solution(15234755161671810769)
XLA Ops:
  0.6 63.8 %crf_backward.1 = (f32[21,16,128]{2,1,0:T(8,128)}, f32[64,16,128]{2,1,0:T(8,128)}, f32[21,21]{1,0:T(8,128)}) custom-call(f32[21,16,128]{2,1,0:T(8,128)} %u_hbm.1, bf16[64,16,128]{2,1,0:T(8,128)(2,1)} %f_hbm.1, f32[21,21]{1,0:T(8,128)} %cm.1, f32[21,16,128]{2,1,0:T(8,128)} %g_hbm.1), custom_call_target="tpu_custom_call" | custom-call | tf_op jit(solution)/shard_map/crf_backward/pallas_call | solution.py:447
  64.5 1.6 %copy.10 = f32[21,16,128]{2,1,0:T(8,128)} copy(f32[21,16,128]{2,1,0:T(8,128)} %get-tuple-element.6) | data formatting | bytes 344064
  66.1 0.0 copy-start
  66.1 1.9 %copy.11 = f32[64,16,128]{2,1,0:T(8,128)} copy(f32[64,16,128]{2,1,0:T(8,128)} %get-tuple-element.7) | data formatting | bytes 1048576
  68.0 0.0 copy-done
  68.0 0.6 copy.12
Async XLA Ops:
  66.1 1.9 %copy-start = (f32[21,21]{1,0:T(8,128)S(1)}, f32[21,21]{1,0:T(8,128)}, u32[]{:S(2)}) copy-start(f32[21,21]{1,0:T(8,128)} %get-tuple-element.8) | copy-start | bytes 5296

commit v2 on v1

--- a/solution.py
+++ b/solution.py
@@ -217,13 +217,15 @@
     for group in range(feats // F_GROUP):
         strip = f_strip[group, height - 3:height - 3 + WIN]
 
-        def f_turn(k, carry, group=group):
-            ch = group * F_GROUP + k
-            edge = pltpu.roll(f_strip[group, height - 3:height - 3 + WIN], LANES - 3 - 6 * k, 1)
-            turn(edge, f_plane[ch, TOP - 3:TOP - 3 + WIN, :], f_shift, ch)
+        def f_turn(i, carry, group=group, strip=strip):
+            for extra in range(8):
+                k = 8 * i + extra
+                ch = group * F_GROUP + k
+                edge = pltpu.roll(strip, LANES - 3 - 6 * k, 1)
+                turn(edge, f_plane[ch, TOP - 3:TOP - 3 + WIN, :], f_shift, ch)
             return carry
 
-        lax.fori_loop(0, F_GROUP, f_turn, 0)
+        lax.fori_loop(0, F_GROUP // 8, f_turn, 0)
 
     factor = 1.0 / (2.0 * feats)
     spread = 1.0 / (2.0 * THETA_PIXELS * THETA_PIXELS)
@@ -233,8 +235,8 @@
 
     def affinity(bi, carry):
         def channels(i, acc):
-            for extra in range(4):
-                ch = 4 * i + extra
+            for extra in range(8):
+                ch = 8 * i + extra
                 center = f_shift[REACH, ch, rows_at(REACH), :]
                 new = []
                 for a in range(SPAN):
@@ -244,7 +246,7 @@
             return acc
 
         zero = jnp.zeros((height, LANES), f32)
-        acc = lax.fori_loop(0, feats // 4, channels, (zero,) * SPAN)
+        acc = lax.fori_loop(0, feats // 8, channels, (zero,) * SPAN)
         step = (bi - REACH).astype(f32)
         for a in range(SPAN):
             away = ((a - REACH) * (a - REACH) + step * step) * spread
@@ -262,13 +264,13 @@
         strip = jnp.where(from_left, rstrip[k, 0, TOP - 3:TOP - 3 + WIN], rstrip[k, 1, TOP - 3:TOP - 3 + WIN])
 
         def f_turn(i, carry):
-            for extra in range(3):
-                ch = 3 * i + extra
+            for extra in range(7):
+                ch = 7 * i + extra
                 edge = pltpu.roll(strip, LANES - 3 - 6 * ch, 1)
                 turn(edge, plane[ch, TOP - 3:TOP - 3 + WIN, :], shift.at[k], ch)
             return carry
 
-        lax.fori_loop(0, classes // 3, f_turn, 0)
+        lax.fori_loop(0, classes // 7, f_turn, 0)
 
     def spread_out(k, dst):
         for block in range(classes // 7):
@@ -282,15 +284,19 @@
             dst[chans] = lax.fori_loop(0, SPAN, step, jnp.zeros((7, height, LANES), f32))
 
     def mix(transposed, source, finish):
-        def one(ch, carry):
-            acc = jnp.zeros((height, LANES), f32)
+        def block(i, carry):
+            acc = [jnp.zeros((height, LANES), f32)] * 7
             for d in range(classes):
-                weight = cm[d, ch] if transposed else cm[ch, d]
-                acc = acc + weight * source[d]
-            finish(ch, acc)
+                value = source[d]
+                for j in range(7):
+                    ch = 7 * i + j
+                    weight = cm[d, ch] if transposed else cm[ch, d]
+                    acc[j] = acc[j] + weight * value
+            for j in range(7):
+                finish(7 * i + j, acc[j])
             return carry
 
-        lax.fori_loop(0, classes, one, 0)
+        lax.fori_loop(0, classes // 7, block, 0)
 
     def set_logits(t):
         def finish(ch, acc):
@@ -370,8 +376,8 @@
     def pair(k_prob, k_grad, finish):
         def one(bi, carry):
             def channels(i, acc):
-                for extra in range(3):
-                    ch = 3 * i + extra
+                for extra in range(7):
+                    ch = 7 * i + extra
                     p_own = shift[k_prob, REACH, ch, rows_at(REACH), :]
                     m_own = shift[k_grad, REACH, ch, rows_at(REACH), :]
                     acc = tuple(
@@ -383,7 +389,7 @@
                 return acc
 
             zero = jnp.zeros((height, LANES), f32)
-            acc = lax.fori_loop(0, classes // 3, channels, (zero,) * SPAN)
+            acc = lax.fori_loop(0, classes // 7, channels, (zero,) * SPAN)
             for a in range(SPAN):
                 finish(bi * SPAN + a, acc[a])
             return carry
@@ -409,20 +415,21 @@
     ug_ref[...] = lgrad[1] + lgrad[0] + softmax_grad(prob[0], ug_ref[...])
     pair(0, 3, close)
 
+    weight_sum = jnp.sum(coef[...], axis=0)
+
     def feature_block(i, carry):
-        base = 4 * i
-        chans = pl.ds(base, 4)
-        center = f_shift[REACH, chans, rows_at(REACH), :]
+        chans = pl.ds(8 * i, 8)
 
         def step(bi, acc):
             for a in range(SPAN):
-                acc = acc + coef[bi * SPAN + a][None] * (f_shift[bi, chans, rows_at(a), :] - center)
+                acc = acc + coef[bi * SPAN + a][None] * f_shift[bi, chans, rows_at(a), :]
             return acc
 
-        fg_ref[chans] = lax.fori_loop(0, SPAN, step, jnp.zeros((4, height, LANES), f32))
+        start = -weight_sum[None] * f_shift[REACH, chans, rows_at(REACH), :]
+        fg_ref[chans] = lax.fori_loop(0, SPAN, step, start)
         return carry
 
-    lax.fori_loop(0, feats // 4, feature_block, 0)
+    lax.fori_loop(0, feats // 8, feature_block, 0)
 
     for k in range(1, n_cols):
         reduce_arrival(1, k).wait_recv()

time: 68.8 us -> 59.8 us (0.87)
  Pallas kernels: 63.8 us -> 54.9 us
    pallas_call x1, Pallas kernels: 63.8 us -> 54.9 us  [on_device(): pl.pallas_call(functools.partial(kernel, n_rows, n_cols, classes, feats),...]
where the time goes in v2:
time: 59.8 us; the launch traced here: 59.6 us
  Pallas kernels  54.9 us (92%)
  local copies, waits for them, and re-layouts  4.08 us (7%)
  between operations  0.64 us (1%)
    pallas_call x1, Pallas kernels, on_device(): pl.pallas_call(functools.partial(kernel, n_rows, n_cols, classes, feats),...  54.9 us
    unnamed x5, local copies, waits for them, and re-layouts  4.08 us

profile of v2, /device:TPU:1, one launch (start us, length us, event | category | flops | bytes accessed | tf_op | source)
XLA Modules:
  0.0 59.6 jit_solution(9507277843518613134)
XLA Ops:
  0.6 54.9 %crf_backward.1 = (f32[21,16,128]{2,1,0:T(8,128)}, f32[64,16,128]{2,1,0:T(8,128)}, f32[21,21]{1,0:T(8,128)}) custom-call(f32[21,16,128]{2,1,0:T(8,128)} %u_hbm.1, bf16[64,16,128]{2,1,0:T(8,128)(2,1)} %f_hbm.1, f32[21,21]{1,0:T(8,128)} %cm.1, f32[21,16,128]{2,1,0:T(8,128)} %g_hbm.1), custom_call_target="tpu_custom_call" | custom-call | tf_op jit(solution)/shard_map/crf_backward/pallas_call | solution.py:454
  55.5 1.6 %copy.10 = f32[21,16,128]{2,1,0:T(8,128)} copy(f32[21,16,128]{2,1,0:T(8,128)} %get-tuple-element.6) | data formatting | bytes 344064
  57.1 0.0 copy-start
  57.1 1.9 %copy.11 = f32[64,16,128]{2,1,0:T(8,128)} copy(f32[64,16,128]{2,1,0:T(8,128)} %get-tuple-element.7) | data formatting | bytes 1048576
  59.0 0.0 copy-done
  59.0 0.6 %copy.12 = f32[21,21]{1,0:T(8,128)} copy(f32[21,21]{1,0:T(8,128)S(1)} %copy-done) | data formatting | bytes 3528
Async XLA Ops:
  57.1 1.9 %copy-start = (f32[21,21]{1,0:T(8,128)S(1)}, f32[21,21]{1,0:T(8,128)}, u32[]{:S(2)}) copy-start(f32[21,21]{1,0:T(8,128)} %get-tuple-element.8) | copy-start | bytes 5296
